TPU v7x, 32 devices: a whole 2x2x4 slice. The times are simulated.
32 devices in a mesh: scene: 4 (over y, x), row: 4 (over z), col: 2 (over core).
Axes of the slice: x: 2, y: 2, z: 4, core: 2. Of those that a mesh axis runs over, the one named last changes fastest.
Arguments:
- scenes: bfloat16 [4, 256, 128, 128], P('scene', 'row', 'col'), may hold values from -6 to 6
- cotangent: bfloat16 [4, 256, 128, 128], P('scene', 'row', 'col'), may hold values from -0.016479492 to 0.016479492
- params: float32 [294912], P(('scene', 'row', 'col')), may hold values from -0.1875 to 0.1875
- partials: float32 [32, 294912], P(('scene', 'row', 'col')), may hold values from -8 to 8
Outputs:
- sam_grad: float32 [294912], P(('scene', 'row', 'col'))
All inputs are finite; a program needn't handle non-finite values.
Results may differ from a plain program's by a relative error of at most 0.0042.
Values may be sent and summed in bfloat16 or wider, within the bound.
A program may use at most 64 MiB of HBM per device.

v0:
```python
import jax
import jax.numpy as jnp
from jax import lax
from jax.sharding import PartitionSpec as P

radius = 2.0
epsilon = 1e-06


def with_halo(cells, sides, width):
    for axis, dim in sides:
        count = lax.axis_size(axis)
        ends = count - 1
        head = lax.slice_in_dim(cells, 0, width, axis=dim)
        tail = lax.slice_in_dim(cells, cells.shape[dim] - width, cells.shape[dim], axis=dim)
        cells = jnp.concatenate(
            [
                lax.ppermute(tail, axis, [(i, (i + 1) % count) for i in range(ends)]),
                cells,
                lax.ppermute(head, axis, [((i + 1) % count, i) for i in range(ends)]),
            ],
            axis=dim,
        )
    return cells


def convolve(padded, kernel):
    return lax.conv_general_dilated(
        padded,
        kernel,
        (1, 1),
        "VALID",
        dimension_numbers=("NHWC", "HWIO", "NHWC"),
        preferred_element_type=jnp.float32,
    )


def widened(field):
    return with_halo(field, (("row", 1), ("col", 2)), 1)


def kernel_grad(padded, errors):
    height = errors.shape[1]
    width = errors.shape[2]
    rows_out = []
    for row_off in range(3):
        cols_out = []
        for col_off in range(3):
            window = padded[:, row_off : row_off + height, col_off : col_off + width, :]
            cols_out.append(
                jnp.einsum("nhwc,nhwd->cd", window, errors, preferred_element_type=jnp.float32)
            )
        rows_out.append(jnp.stack(cols_out))
    return jnp.stack(rows_out)


def on_device(scenes, cotangent, params, partials):
    local_part = partials[0]
    totals = lax.psum(local_part, ("scene", "row", "col"))
    raw_whole = lax.all_gather(params, ("scene", "row", "col"), axis=0, tiled=True)
    factor = radius / (jnp.sqrt(jnp.sum(totals * totals)) + epsilon)
    whole = (raw_whole + factor * totals).astype(jnp.bfloat16)
    channels = scenes.shape[3]
    kernels = whole.reshape(2, 3, 3, channels, channels)
    kernel_one = kernels[0]
    flipped = jnp.transpose(kernels[1][::-1, ::-1], (0, 1, 3, 2))
    padded_in = widened(scenes)
    pre = convolve(padded_in, kernel_one)
    hidden = jax.nn.silu(pre).astype(jnp.bfloat16)
    back = convolve(widened(cotangent), flipped)
    squash = jax.nn.sigmoid(pre)
    delta = (back * squash * (1.0 + pre * (1.0 - squash))).astype(jnp.bfloat16)
    grad_one = kernel_grad(padded_in, delta)
    grad_two = kernel_grad(widened(hidden), cotangent)
    local_grad = jnp.stack([grad_one, grad_two]).reshape(-1)
    return lax.psum_scatter(local_grad, ("scene", "row", "col"), scatter_dimension=0, tiled=True)


def solution(mesh):
    return jax.shard_map(
        on_device,
        mesh=mesh,
        in_specs=(
            P("scene", "row", "col", None),
            P("scene", "row", "col", None),
            P(("scene", "row", "col")),
            P(("scene", "row", "col"), None),
        ),
        out_specs=P(("scene", "row", "col")),
        check_vma=False,
    )
```

profile of v0, /device:TPU:0, one launch (start us, length us, event | category | flops | bytes accessed | tf_op | source)
XLA Modules:
  0.0 384.6 jit_solution(3427847306633833855)
XLA Ops:
  8.1 5.1 %collective-permute-start = (bf16[1,1,64,128]{3,2,1,0:T(8,128)(2,1)S(1)}, bf16[1,1,64,128]{3,2,1,0:T(8,128)(2,1)S(1)}, u32[]{:S(2)}, u32[]{:S(2)}) collective-permute-start(bf16[1,1,64,128]{3,2,1,0:T(8,128)(2,1)S(1)} %get-tuple-element.18), channel_id=1, source_target_pairs={{0,2},{2,4},{4,6},{1,3},{3,5},{5,7},{8,10},{10,12},{12,14},{9,11},... | collective-permute-start | bytes 49160 | tf_op jit(solution)/shard_map/ppermute | solution.py:18
  13.2 1.3 collective-permute-start.1
  15.2 4.5 %collective-permute-start.3 = (bf16[1,1,64,128]{3,2,1,0:T(8,128)(2,1)S(1)}, bf16[1,1,64,128]{3,2,1,0:T(8,128)(2,1)S(1)}, u32[]{:S(2)}, u32[]{:S(2)}) collective-permute-start(bf16[1,1,64,128]{3,2,1,0:T(8,128)(2,1)S(1)} %get-tuple-element.16), channel_id=1, source_target_pairs={{0,2},{2,4},{4,6},{1,3},{3,5},{5,7},{8,10},{10,12},{12,14},{9,11},... | collective-permute-start | bytes 49160 | tf_op jit(solution)/shard_map/ppermute | solution.py:18
  19.8 1.3 collective-permute-start.4
  22.5 1.3 collective-permute-start.2
  23.8 1.3 collective-permute-start.7
  25.5 2.9 collective-permute-start.5
  28.4 1.3 collective-permute-start.6
  34.5 112.6 %all-reduce.4.cloned.1.call-done = f32[294912]{0:T(1024)} async-done(((f32[294912]{0:T(1024)}), f32[294912]{0:T(1024)}) %all-reduce.4.cloned.1.call-update) | async-done | bytes 1179664 | tf_op jit(solution)/shard_map/psum | solution.py:59
  147.1 2.3 multiply_reduce_fusion
  150.2 53.1 %all-gather.2.cloned.1.call-done = f32[294912]{0:T(1024)} async-done(((f32[9216]{0:T(1024)}), f32[294912]{0:T(1024)}) %all-gather.2.cloned.1.call-update) | async-done | bytes 1179664 | tf_op jit(solution)/shard_map/all_gather | solution.py:60
  203.2 1.5 add_convert_fusion
  204.8 3.2 multiply_convert_fusion.1
  209.4 3.4 multiply_convert_fusion
  213.2 1.1 copy-done.4
  214.4 1.3 convolution_bitcast_fusion.13
  215.8 2.5 collective-permute-start.8
  218.4 1.6 collective-permute-start.9
  220.0 2.1 convolution_bitcast_fusion.4
  222.1 1.4 convolution_bitcast_fusion.11
  223.5 1.4 convolution_bitcast_fusion.9
  224.9 1.3 convolution_bitcast_fusion.10
  226.2 1.4 convolution_bitcast_fusion.14
  227.6 1.4 convolution_bitcast_fusion.12
  229.0 1.4 convolution_bitcast_fusion.17
  230.4 1.4 convolution_bitcast_fusion.15
  231.8 1.3 convolution_bitcast_fusion.16
  234.3 1.8 collective-permute-start.10
  236.1 1.3 collective-permute-start.11
  243.1 1.1 pad_maximum_fusion.1
  244.2 132.5 %all-reduce.6.cloned.1.call-done = f32[294912]{0:T(1024)} async-done(((f32[294912]{0:T(1024)}), f32[294912]{0:T(1024)}) %all-reduce.6.cloned.1.call-update) | async-done | bytes 1179664
  376.7 1.4 dynamic-slice
  (98 shorter events, 17.2 us)
Async XLA Ops:
  6.5 1.5 copy-start.3
  6.5 140.6 %all-reduce.4.cloned.1.call-start = ((), (), s32[]{:S(2)}) async-start(), calls=%async_computation.1 | async-start | bytes 2359296 | tf_op jit(solution)/shard_map/psum | solution.py:59
  7.3 196.0 %all-gather.2.cloned.1.call-start = ((), (), s32[]{:S(2)}) async-start(), calls=%async_computation | async-start | bytes 1216512 | tf_op jit(solution)/shard_map/all_gather | solution.py:60
  8.0 368.7 %all-reduce.6.cloned.1.call-start = ((), (), s32[]{:S(2)}) async-start(), calls=%async_computation.2 | async-start | bytes 2359296
  8.1 17.1 %copy-start.5 = (bf16[1,64,64,128]{3,2,1,0:T(8,128)(2,1)S(1)}, bf16[1,64,64,128]{3,2,1,0:T(8,128)(2,1)}, u32[]{:S(2)}) copy-start(bf16[1,64,64,128]{3,2,1,0:T(8,128)(2,1)} %param.5) | copy-start | bytes 3145732
  8.1 13.0 %collective-permute-start = (bf16[1,1,64,128]{3,2,1,0:T(8,128)(2,1)S(1)}, bf16[1,1,64,128]{3,2,1,0:T(8,128)(2,1)S(1)}, u32[]{:S(2)}, u32[]{:S(2)}) collective-permute-start(bf16[1,1,64,128]{3,2,1,0:T(8,128)(2,1)S(1)} %get-tuple-element.18), channel_id=1, source_target_pairs={{0,2},{2,4},{4,6},{1,3},{3,5},{5,7},{8,10},{10,12},{12,14},{9,11},... | collective-permute-start | bytes 49160 | tf_op jit(solution)/shard_map/ppermute | solution.py:18
  13.2 8.6 %collective-permute-start.1 = (bf16[1,1,64,128]{3,2,1,0:T(8,128)(2,1)S(1)}, bf16[1,1,64,128]{3,2,1,0:T(8,128)(2,1)S(1)}, u32[]{:S(2)}, u32[]{:S(2)}) collective-permute-start(bf16[1,1,64,128]{3,2,1,0:T(8,128)(2,1)S(1)} %get-tuple-element.17), channel_id=1, source_target_pairs={{2,0},{4,2},{6,4},{3,1},{5,3},{7,5},{10,8},{12,10},{14,12},{11,9},... | collective-permute-start | bytes 49160 | tf_op jit(solution)/shard_map/ppermute | solution.py:20
  15.2 9.9 %collective-permute-start.3 = (bf16[1,1,64,128]{3,2,1,0:T(8,128)(2,1)S(1)}, bf16[1,1,64,128]{3,2,1,0:T(8,128)(2,1)S(1)}, u32[]{:S(2)}, u32[]{:S(2)}) collective-permute-start(bf16[1,1,64,128]{3,2,1,0:T(8,128)(2,1)S(1)} %get-tuple-element.16), channel_id=1, source_target_pairs={{0,2},{2,4},{4,6},{1,3},{3,5},{5,7},{8,10},{10,12},{12,14},{9,11},... | collective-permute-start | bytes 49160 | tf_op jit(solution)/shard_map/ppermute | solution.py:18
  19.8 5.6 %collective-permute-start.4 = (bf16[1,1,64,128]{3,2,1,0:T(8,128)(2,1)S(1)}, bf16[1,1,64,128]{3,2,1,0:T(8,128)(2,1)S(1)}, u32[]{:S(2)}, u32[]{:S(2)}) collective-permute-start(bf16[1,1,64,128]{3,2,1,0:T(8,128)(2,1)S(1)} %get-tuple-element.15), channel_id=1, source_target_pairs={{2,0},{4,2},{6,4},{3,1},{5,3},{7,5},{10,8},{12,10},{14,12},{11,9},... | collective-permute-start | bytes 49160 | tf_op jit(solution)/shard_map/ppermute | solution.py:20
  21.1 0.6 copy-start.11
  21.8 0.6 copy-start.13
  22.5 7.2 %collective-permute-start.2 = (bf16[1,66,1,128]{3,2,1,0:T(2,128)(2,1)S(1)}, bf16[1,66,1,128]{3,2,1,0:T(2,128)(2,1)S(1)}, u32[]{:S(2)}, u32[]{:S(2)}) collective-permute-start(bf16[1,66,1,128]{3,2,1,0:T(2,128)(2,1)S(1)} %get-tuple-element.13), channel_id=1, source_target_pairs={{0,1},{2,3},{4,5},{6,7},{8,9},{10,11},{12,13},{14,15},{16,17},{18,... | collective-permute-start | bytes 50696 | tf_op jit(solution)/shard_map/ppermute | solution.py:18
  23.8 5.9 %collective-permute-start.7 = (bf16[1,66,1,128]{3,2,1,0:T(2,128)(2,1)S(1)}, bf16[1,66,1,128]{3,2,1,0:T(2,128)(2,1)S(1)}, u32[]{:S(2)}, u32[]{:S(2)}) collective-permute-start(bf16[1,66,1,128]{3,2,1,0:T(2,128)(2,1)S(1)} %get-tuple-element.14), channel_id=1, source_target_pairs={{1,0},{3,2},{5,4},{7,6},{9,8},{11,10},{13,12},{15,14},{17,16},{19,... | collective-permute-start | bytes 50696 | tf_op jit(solution)/shard_map/ppermute | solution.py:20
  25.5 6.1 %collective-permute-start.5 = (bf16[1,66,1,128]{3,2,1,0:T(2,128)(2,1)S(1)}, bf16[1,66,1,128]{3,2,1,0:T(2,128)(2,1)S(1)}, u32[]{:S(2)}, u32[]{:S(2)}) collective-permute-start(bf16[1,66,1,128]{3,2,1,0:T(2,128)(2,1)S(1)} %get-tuple-element.7), channel_id=1, source_target_pairs={{0,1},{2,3},{4,5},{6,7},{8,9},{10,11},{12,13},{14,15},{16,17},{18,... | collective-permute-start | bytes 50696 | tf_op jit(solution)/shard_map/ppermute | solution.py:18
  28.4 3.2 collective-permute-start.6
  32.7 1.0 copy-start.1
  147.1 56.1 %copy-start = (f32[294912]{0:T(1024)S(1)}, f32[294912]{0:T(1024)}, u32[]{:S(2)}) copy-start(f32[294912]{0:T(1024)} %all-reduce.4.cloned.1.call-done) | copy-start | bytes 3538948
  150.1 54.7 %copy-start.15 = (pred[8,9]{0,1:T(8,128)(4,1)S(1)}, pred[8,9]{0,1:T(8,128)(4,1)}, u32[]{:S(2)}) copy-start(pred[8,9]{0,1:T(8,128)(4,1)} %constant.21) | copy-start | bytes 220
  203.2 1.6 copy-start.9
  208.1 1.3 copy-start.2
  208.1 1.3 copy-start.10
  213.1 1.2 copy-start.4
  214.4 1.3 copy-start.7
  215.8 18.3 %collective-permute-start.8 = (bf16[1,1,64,128]{3,2,1,0:T(8,128)(2,1)S(1)}, bf16[1,1,64,128]{3,2,1,0:T(8,128)(2,1)S(1)}, u32[]{:S(2)}, u32[]{:S(2)}) collective-permute-start(bf16[1,1,64,128]{3,2,1,0:T(8,128)(2,1)S(1)} %slice.186), channel_id=1, source_target_pairs={{0,2},{2,4},{4,6},{1,3},{3,5},{5,7},{8,10},{10,12},{12,14},{9,11},... | collective-permute-start | bytes 49160 | tf_op jit(solution)/shard_map/ppermute | solution.py:18
  218.3 3.7 copy-start.8
  218.4 15.8 %collective-permute-start.9 = (bf16[1,1,64,128]{3,2,1,0:T(8,128)(2,1)S(1)}, bf16[1,1,64,128]{3,2,1,0:T(8,128)(2,1)S(1)}, u32[]{:S(2)}, u32[]{:S(2)}) collective-permute-start(bf16[1,1,64,128]{3,2,1,0:T(8,128)(2,1)S(1)} %slice.189), channel_id=1, source_target_pairs={{2,0},{4,2},{6,4},{3,1},{5,3},{7,5},{10,8},{12,10},{14,12},{11,9},... | collective-permute-start | bytes 49160 | tf_op jit(solution)/shard_map/ppermute | solution.py:20
  223.5 1.4 copy-start.14
  230.4 1.4 copy-start.12
  233.2 4.2 %copy-start.6 = (bf16[1,64,64,128]{3,2,1,0:T(8,128)(2,1)S(1)}, bf16[1,64,64,128]{3,2,1,0:T(8,128)(2,1)}, u32[]{:S(2)}) copy-start(bf16[1,64,64,128]{3,2,1,0:T(8,128)(2,1)} %param.5) | copy-start | bytes 3145732
  234.3 4.1 %collective-permute-start.10 = (bf16[1,66,1,128]{3,2,1,0:T(2,128)(2,1)S(1)}, bf16[1,66,1,128]{3,2,1,0:T(2,128)(2,1)S(1)}, u32[]{:S(2)}, u32[]{:S(2)}) collective-permute-start(bf16[1,66,1,128]{3,2,1,0:T(2,128)(2,1)S(1)} %get-tuple-element.11), channel_id=1, source_target_pairs={{0,1},{2,3},{4,5},{6,7},{8,9},{10,11},{12,13},{14,15},{16,17},{18,... | collective-permute-start | bytes 50696 | tf_op jit(solution)/shard_map/ppermute | solution.py:18
  236.1 3.1 collective-permute-start.11
Sparse Core Ops, SparseCore 0:
  12.7 134.3 all-reduce.3
  150.1 53.0 all-gather.1
  244.3 132.3 all-reduce.5
where the time goes:
time: 385 us
  waiting for transfers between devices  301 us (78%)
  starting transfers between devices  26.3 us (7%)
  matrix products  24.9 us (6%)
  between operations  14.5 us (4%)
  local copies, waits for them, and re-layouts  11.1 us (3%)
  other arithmetic  7.21 us (2%)
    unnamed x4, waiting for transfers between devices  134 us
    psum x1, waiting for transfers between devices, on_device(): totals = lax.psum(local_part, ('scene', 'row', 'col'))  113 us
    all_gather x1, waiting for transfers between devices, on_device(): lax.all_gather(params, ('scene', 'row', 'col'), axis=0, tiled=True)  53.1 us
    dot_general x18, matrix products, kernel_grad(): jnp.einsum('nhwc,nhwd->cd', window, errors, preferred_element_type=jnp.fl...  18.2 us
    ppermute x6, starting transfers between devices, with_halo(): lax.ppermute(tail, axis, [(i, (i + 1) % count) for i in range(ends)])  18.1 us
    ppermute x6, starting transfers between devices, with_halo(): lax.ppermute(head, axis, [((i + 1) % count, i) for i in range(ends)])  8.06 us
  transfers between devices with their start and end apart: 15, of which 5 were waited for; matrix products, arithmetic and copies ran while one was open for 6% of the time, Pallas kernels for 0%

commit v1 on v0

--- a/solution.py
+++ b/solution.py
@@ -1,3 +1,4 @@
+import functools
 import jax
 import jax.numpy as jnp
 from jax import lax
@@ -5,6 +6,24 @@
 
 radius = 2.0
 epsilon = 1e-06
+
+
+def time_the_numbers(x0, axis_key):
+    arr_next = lax.axis_size(axis_key)
+    r1 = lax.axis_index(axis_key)
+    item_now, h_now = (arr_next, r1)
+    kept_arr, answer = (x0, 1)
+    while answer < item_now:
+        side_arr = tuple(((k, k ^ answer) for k in range(item_now)))
+        outcome_arr = lax.ppermute(kept_arr, axis_key, side_arr)
+        vec_out = jnp.concatenate([kept_arr, outcome_arr], 0)
+        upper = jnp.concatenate([outcome_arr, kept_arr], 0)
+        kept_arr = jnp.where(h_now & answer == 0, vec_out, upper)
+        answer = 2 * answer
+    return kept_arr
+
+
+patches_rest = functools.partial(time_the_numbers, axis_key=("scene", "row", "col"))
 
 
 def with_halo(cells, sides, width):
@@ -57,7 +76,7 @@
 def on_device(scenes, cotangent, params, partials):
     local_part = partials[0]
     totals = lax.psum(local_part, ("scene", "row", "col"))
-    raw_whole = lax.all_gather(params, ("scene", "row", "col"), axis=0, tiled=True)
+    raw_whole = patches_rest(params)
     factor = radius / (jnp.sqrt(jnp.sum(totals * totals)) + epsilon)
     whole = (raw_whole + factor * totals).astype(jnp.bfloat16)
     channels = scenes.shape[3]

time: 385 us -> 334 us (0.87)
  waiting for transfers between devices: 301 us -> 241 us
  starting transfers between devices: 26.3 us -> 35.8 us
    all_gather x1 -> x0, waiting for transfers between devices: 53.1 us -> none  [on_device(): lax.all_gather(params, ('scene', 'row', 'col'), axis=0, tiled=True)]
    psum x1, waiting for transfers between devices: 113 us -> 96.1 us  [on_device(): totals = lax.psum(local_part, ('scene', 'row', 'col'))]
    ppermute x0 -> x5, waiting for transfers between devices: none -> 11.7 us  [time_the_numbers(): outcome_arr = lax.ppermute(kept_arr, axis_key, side_arr)]
    ppermute x0 -> x5, starting transfers between devices: none -> 9.15 us  [time_the_numbers(): outcome_arr = lax.ppermute(kept_arr, axis_key, side_arr)]
    unnamed x4 -> x3, waiting for transfers between devices: 134 us -> 132 us
  transfers between devices with their start and end apart: 15 -> 19, of which waited for: 5 -> 6; matrix products, arithmetic and copies ran while one was open for 6% -> 6% of each run, Pallas kernels for 0% -> 0%
where the time goes in v1:
time: 334 us; the launch traced here: 333 us
  waiting for transfers between devices  241 us (72%)
  starting transfers between devices  35.8 us (11%)
  matrix products  23.7 us (7%)
  between operations  14.9 us (4%)
  local copies, waits for them, and re-layouts  10.5 us (3%)
  other arithmetic  7.24 us (2%)
    unnamed x3, waiting for transfers between devices  132 us
    psum x1, waiting for transfers between devices, on_device(): totals = lax.psum(local_part, ('scene', 'row', 'col'))  96.1 us
    ppermute x6, starting transfers between devices, with_halo(): lax.ppermute(tail, axis, [(i, (i + 1) % count) for i in range(ends)])  18.6 us
    dot_general x18, matrix products, kernel_grad(): jnp.einsum('nhwc,nhwd->cd', window, errors, preferred_element_type=jnp.fl...  17 us
    ppermute x5, waiting for transfers between devices, time_the_numbers(): outcome_arr = lax.ppermute(kept_arr, axis_key, side_arr)  11.7 us
    ppermute x5, starting transfers between devices, time_the_numbers(): outcome_arr = lax.ppermute(kept_arr, axis_key, side_arr)  9.15 us
    ppermute x6, starting transfers between devices, with_halo(): lax.ppermute(head, axis, [((i + 1) % count, i) for i in range(ends)])  8.06 us
    unnamed x46, local copies, waits for them, and re-layouts  7.33 us
  transfers between devices with their start and end apart: 19, of which 6 were waited for; matrix products, arithmetic and copies ran while one was open for 6% of the time, Pallas kernels for 0%

profile of v1, /device:TPU:0, one launch (start us, length us, event | category | flops | bytes accessed | tf_op | source)
XLA Modules:
  0.0 332.9 jit_solution(14596863011184020188)
XLA Ops:
  8.1 4.9 %collective-permute-start = (bf16[1,1,64,128]{3,2,1,0:T(8,128)(2,1)S(1)}, bf16[1,1,64,128]{3,2,1,0:T(8,128)(2,1)S(1)}, u32[]{:S(2)}, u32[]{:S(2)}) collective-permute-start(bf16[1,1,64,128]{3,2,1,0:T(8,128)(2,1)S(1)} %get-tuple-element.18), channel_id=1, source_target_pairs={{0,2},{2,4},{4,6},{1,3},{3,5},{5,7},{8,10},{10,12},{12,14},{9,11},... | collective-permute-start | bytes 49160 | tf_op jit(solution)/shard_map/ppermute | solution.py:37
  13.0 1.3 collective-permute-start.1
  15.0 4.5 %collective-permute-start.3 = (bf16[1,1,64,128]{3,2,1,0:T(8,128)(2,1)S(1)}, bf16[1,1,64,128]{3,2,1,0:T(8,128)(2,1)S(1)}, u32[]{:S(2)}, u32[]{:S(2)}) collective-permute-start(bf16[1,1,64,128]{3,2,1,0:T(8,128)(2,1)S(1)} %get-tuple-element.16), channel_id=1, source_target_pairs={{0,2},{2,4},{4,6},{1,3},{3,5},{5,7},{8,10},{10,12},{12,14},{9,11},... | collective-permute-start | bytes 49160 | tf_op jit(solution)/shard_map/ppermute | solution.py:37
  19.6 1.3 collective-permute-start.4
  21.1 2.7 collective-permute-start.8
  23.9 2.5 collective-permute-done.8
  26.4 3.0 collective-permute-start.9
  29.5 1.3 collective-permute-start.12
  30.8 3.0 collective-permute-start.2
  33.8 2.6 collective-permute-done.9
  36.4 1.5 collective-permute-start.10
  38.2 6.5 %collective-permute-done.10 = f32[73728]{0:T(1024)S(1)} collective-permute-done((f32[73728]{0:T(1024)S(1)}, f32[73728]{0:T(1024)S(1)}, u32[]{:S(2)}, u32[]{:S(2)}) %collective-permute-start.10) | collective-permute-done | bytes 294944 | tf_op jit(solution)/shard_map/ppermute | solution.py:18
  44.7 1.4 collective-permute-start.11
  46.2 1.3 collective-permute-start.5
  47.5 1.3 collective-permute-start.6
  53.5 96.1 %all-reduce.4.cloned.1.call-done = f32[294912]{0:T(1024)} async-done(((f32[294912]{0:T(1024)}), f32[294912]{0:T(1024)}) %all-reduce.4.cloned.1.call-update) | async-done | bytes 1179664 | tf_op jit(solution)/shard_map/psum | solution.py:78
  149.6 2.2 multiply_reduce_fusion
  152.5 1.5 fusion.16
  154.0 3.2 multiply_convert_fusion.1
  158.6 3.4 %multiply_convert_fusion = bf16[64,8,9,128]{3,1,2,0:T(8,128)(2,1)S(1)} fusion(f32[64,8,9,128]{3,1,2,0:T(8,128)S(1)} %get-tuple-element.22, bf16[3,3,128,128]{3,2,1,0:T(8,128)(2,1)S(1)} %bitcast.192, bf16[66,1,7,2,128]{4,2,3,0,1:T(8,128)(2,1)S(1)} %slice.173, bf16[66,1,8,9,128]{4,2,3,0,1:T(8,128)(2,1)S(1)} %copy-done.2, pred[8,9]{0,1:T(8,128)(4,1)S(1)} %copy-done.18), kind=kOutput, calls=%fused_computation.3 | convolution fusion | flops 1369903104 | bytes 5286984 | tf_op jit(solution)/shard_map/conv_general_dilated | solution.py:47
  163.6 1.3 convolution_bitcast_fusion.13
  165.0 3.5 %collective-permute-start.13 = (bf16[1,1,64,128]{3,2,1,0:T(8,128)(2,1)S(1)}, bf16[1,1,64,128]{3,2,1,0:T(8,128)(2,1)S(1)}, u32[]{:S(2)}, u32[]{:S(2)}) collective-permute-start(bf16[1,1,64,128]{3,2,1,0:T(8,128)(2,1)S(1)} %slice.186), channel_id=1, source_target_pairs={{0,2},{2,4},{4,6},{1,3},{3,5},{5,7},{8,10},{10,12},{12,14},{9,11},... | collective-permute-start | bytes 49160 | tf_op jit(solution)/shard_map/ppermute | solution.py:37
  168.6 1.6 collective-permute-start.14
  171.2 1.4 convolution_bitcast_fusion.11
  173.9 1.4 convolution_bitcast_fusion.9
  175.3 1.4 convolution_bitcast_fusion.14
  176.7 1.4 convolution_bitcast_fusion.12
  178.1 1.4 convolution_bitcast_fusion.17
  179.5 1.4 convolution_bitcast_fusion.15
  183.3 1.3 collective-permute-start.15
  192.7 131.9 %all-reduce.6.cloned.1.call-done = f32[294912]{0:T(1024)} async-done(((f32[294912]{0:T(1024)}), f32[294912]{0:T(1024)}) %all-reduce.6.cloned.1.call-update) | async-done | bytes 1179664
  324.7 1.4 dynamic-slice
  (115 shorter events, 22.8 us)
Async XLA Ops:
  6.5 14.4 %copy-start.5 = (bf16[1,64,64,128]{3,2,1,0:T(8,128)(2,1)S(1)}, bf16[1,64,64,128]{3,2,1,0:T(8,128)(2,1)}, u32[]{:S(2)}) copy-start(bf16[1,64,64,128]{3,2,1,0:T(8,128)(2,1)} %param.4) | copy-start | bytes 3145732
  6.5 143.0 %all-reduce.4.cloned.1.call-start = ((), (), s32[]{:S(2)}) async-start(), calls=%async_computation | async-start | bytes 2359296 | tf_op jit(solution)/shard_map/psum | solution.py:78
  6.5 14.6 %collective-permute-start.7 = (f32[9216]{0:T(1024)}, f32[9216]{0:T(1024)S(1)}, u32[]{:S(2)}, u32[]{:S(2)}) collective-permute-start(f32[9216]{0:T(1024)} %param.6), channel_id=1, source_target_pairs={{0,1},{1,0},{2,3},{3,2},{4,5},{5,4},{6,7},{7,6},{8,9},{9,8},{10,11... | collective-permute-start | bytes 110600 | tf_op jit(solution)/shard_map/ppermute | solution.py:18
  7.3 13.9 %copy-start.11 = (f32[9216]{0:T(1024)S(1)}, f32[9216]{0:T(1024)}, u32[]{:S(2)}) copy-start(f32[9216]{0:T(1024)} %param.6) | copy-start | bytes 110596
  7.3 317.4 %all-reduce.6.cloned.1.call-start = ((), (), s32[]{:S(2)}) async-start(), calls=%async_computation.1 | async-start | bytes 2359296
  8.1 12.9 %collective-permute-start = (bf16[1,1,64,128]{3,2,1,0:T(8,128)(2,1)S(1)}, bf16[1,1,64,128]{3,2,1,0:T(8,128)(2,1)S(1)}, u32[]{:S(2)}, u32[]{:S(2)}) collective-permute-start(bf16[1,1,64,128]{3,2,1,0:T(8,128)(2,1)S(1)} %get-tuple-element.18), channel_id=1, source_target_pairs={{0,2},{2,4},{4,6},{1,3},{3,5},{5,7},{8,10},{10,12},{12,14},{9,11},... | collective-permute-start | bytes 49160 | tf_op jit(solution)/shard_map/ppermute | solution.py:37
  13.0 10.8 %collective-permute-start.1 = (bf16[1,1,64,128]{3,2,1,0:T(8,128)(2,1)S(1)}, bf16[1,1,64,128]{3,2,1,0:T(8,128)(2,1)S(1)}, u32[]{:S(2)}, u32[]{:S(2)}) collective-permute-start(bf16[1,1,64,128]{3,2,1,0:T(8,128)(2,1)S(1)} %get-tuple-element.17), channel_id=1, source_target_pairs={{2,0},{4,2},{6,4},{3,1},{5,3},{7,5},{10,8},{12,10},{14,12},{11,9},... | collective-permute-start | bytes 49160 | tf_op jit(solution)/shard_map/ppermute | solution.py:39
  15.0 22.9 %collective-permute-start.3 = (bf16[1,1,64,128]{3,2,1,0:T(8,128)(2,1)S(1)}, bf16[1,1,64,128]{3,2,1,0:T(8,128)(2,1)S(1)}, u32[]{:S(2)}, u32[]{:S(2)}) collective-permute-start(bf16[1,1,64,128]{3,2,1,0:T(8,128)(2,1)S(1)} %get-tuple-element.16), channel_id=1, source_target_pairs={{0,2},{2,4},{4,6},{1,3},{3,5},{5,7},{8,10},{10,12},{12,14},{9,11},... | collective-permute-start | bytes 49160 | tf_op jit(solution)/shard_map/ppermute | solution.py:37
  19.6 18.5 %collective-permute-start.4 = (bf16[1,1,64,128]{3,2,1,0:T(8,128)(2,1)S(1)}, bf16[1,1,64,128]{3,2,1,0:T(8,128)(2,1)S(1)}, u32[]{:S(2)}, u32[]{:S(2)}) collective-permute-start(bf16[1,1,64,128]{3,2,1,0:T(8,128)(2,1)S(1)} %get-tuple-element.15), channel_id=1, source_target_pairs={{2,0},{4,2},{6,4},{3,1},{5,3},{7,5},{10,8},{12,10},{14,12},{11,9},... | collective-permute-start | bytes 49160 | tf_op jit(solution)/shard_map/ppermute | solution.py:39
  20.9 17.0 %copy-start.7 = (bf16[1,64,64,128]{3,2,1,0:T(8,128)(2,1)S(1)}, bf16[1,64,64,128]{3,2,1,0:T(8,128)(2,1)}, u32[]{:S(2)}) copy-start(bf16[1,64,64,128]{3,2,1,0:T(8,128)(2,1)} %param.5) | copy-start | bytes 3145732
  21.1 5.2 %collective-permute-start.8 = (f32[18432]{0:T(1024)S(1)}, f32[18432]{0:T(1024)S(1)}, u32[]{:S(2)}, u32[]{:S(2)}) collective-permute-start(f32[18432]{0:T(1024)S(1)} %maximum_select_fusion.4), channel_id=1, source_target_pairs={{0,2},{1,3},{2,0},{3,1},{4,6},{5,7},{6,4},{7,5},{8,10},{9,11},{10,... | collective-permute-start | bytes 221192 | tf_op jit(solution)/shard_map/ppermute | solution.py:18
  23.9 14.3 %copy-start.16 = (bf16[1,1,64,128]{3,2,1,0:T(8,128)(2,1)}, bf16[1,1,64,128]{3,2,1,0:T(8,128)(2,1)S(1)}, u32[]{:S(2)}) copy-start(bf16[1,1,64,128]{3,2,1,0:T(8,128)(2,1)S(1)} %collective-permute-done.1) | copy-start | bytes 49156
  23.9 25.0 %copy-start.3 = (bf16[1,66,64,128]{3,2,1,0:T(8,128)(2,1)}, bf16[1,66,64,128]{3,2,1,0:T(8,128)(2,1)S(1)}, u32[]{:S(2)}) copy-start(bf16[1,66,64,128]{3,2,1,0:T(8,128)(2,1)S(1)} %constant_dynamic-update-slice_fusion) | copy-start | bytes 3244036
  26.4 10.0 %collective-permute-start.9 = (f32[36864]{0:T(1024)S(1)}, f32[36864]{0:T(1024)S(1)}, u32[]{:S(2)}, u32[]{:S(2)}) collective-permute-start(f32[36864]{0:T(1024)S(1)} %maximum_select_fusion.3), channel_id=1, source_target_pairs={{0,4},{1,5},{2,6},{3,7},{4,0},{5,1},{6,2},{7,3},{8,12},{9,13},{10,... | collective-permute-start | bytes 442376 | tf_op jit(solution)/shard_map/ppermute | solution.py:18
  29.5 19.4 %collective-permute-start.12 = (bf16[1,66,1,128]{3,2,1,0:T(2,128)(2,1)S(1)}, bf16[1,66,1,128]{3,2,1,0:T(2,128)(2,1)S(1)}, u32[]{:S(2)}, u32[]{:S(2)}) collective-permute-start(bf16[1,66,1,128]{3,2,1,0:T(2,128)(2,1)S(1)} %get-tuple-element.14), channel_id=1, source_target_pairs={{1,0},{3,2},{5,4},{7,6},{9,8},{11,10},{13,12},{15,14},{17,16},{19,... | collective-permute-start | bytes 50696 | tf_op jit(solution)/shard_map/ppermute | solution.py:39
  30.8 18.1 %collective-permute-start.2 = (bf16[1,66,1,128]{3,2,1,0:T(2,128)(2,1)S(1)}, bf16[1,66,1,128]{3,2,1,0:T(2,128)(2,1)S(1)}, u32[]{:S(2)}, u32[]{:S(2)}) collective-permute-start(bf16[1,66,1,128]{3,2,1,0:T(2,128)(2,1)S(1)} %get-tuple-element.13), channel_id=1, source_target_pairs={{0,1},{2,3},{4,5},{6,7},{8,9},{10,11},{12,13},{14,15},{16,17},{18,... | collective-permute-start | bytes 50696 | tf_op jit(solution)/shard_map/ppermute | solution.py:37
  36.4 8.3 %collective-permute-start.10 = (f32[73728]{0:T(1024)S(1)}, f32[73728]{0:T(1024)S(1)}, u32[]{:S(2)}, u32[]{:S(2)}) collective-permute-start(f32[73728]{0:T(1024)S(1)} %maximum_select_fusion.2), channel_id=1, source_target_pairs={{0,8},{1,9},{2,10},{3,11},{4,12},{5,13},{6,14},{7,15},{8,0},{9,1},... | collective-permute-start | bytes 884744 | tf_op jit(solution)/shard_map/ppermute | solution.py:18
  44.7 107.7 %collective-permute-start.11 = (f32[147456]{0:T(1024)S(1)}, f32[147456]{0:T(1024)}, u32[]{:S(2)}, u32[]{:S(2)}) collective-permute-start(f32[147456]{0:T(1024)S(1)} %maximum_select_fusion.1), channel_id=1, source_target_pairs={{0,16},{1,17},{2,18},{3,19},{4,20},{5,21},{6,22},{7,23},{8,24},{9,... | collective-permute-start | bytes 1769480 | tf_op jit(solution)/shard_map/ppermute | solution.py:18
  46.2 5.0 %collective-permute-start.5 = (bf16[1,66,1,128]{3,2,1,0:T(2,128)(2,1)S(1)}, bf16[1,66,1,128]{3,2,1,0:T(2,128)(2,1)S(1)}, u32[]{:S(2)}, u32[]{:S(2)}) collective-permute-start(bf16[1,66,1,128]{3,2,1,0:T(2,128)(2,1)S(1)} %get-tuple-element.7), channel_id=1, source_target_pairs={{0,1},{2,3},{4,5},{6,7},{8,9},{10,11},{12,13},{14,15},{16,17},{18,... | collective-permute-start | bytes 50696 | tf_op jit(solution)/shard_map/ppermute | solution.py:37
  47.5 3.7 %collective-permute-start.6 = (bf16[1,66,1,128]{3,2,1,0:T(2,128)(2,1)S(1)}, bf16[1,66,1,128]{3,2,1,0:T(2,128)(2,1)S(1)}, u32[]{:S(2)}, u32[]{:S(2)}) collective-permute-start(bf16[1,66,1,128]{3,2,1,0:T(2,128)(2,1)S(1)} %get-tuple-element.8), channel_id=1, source_target_pairs={{1,0},{3,2},{5,4},{7,6},{9,8},{11,10},{13,12},{15,14},{17,16},{19,... | collective-permute-start | bytes 50696 | tf_op jit(solution)/shard_map/ppermute | solution.py:39
  149.6 2.9 copy-start
  152.4 1.6 copy-start.18
  163.6 1.3 copy-start.9
  164.9 5.3 %copy-start.8 = (bf16[1,64,64,128]{3,2,1,0:T(8,128)(2,1)S(1)}, bf16[1,64,64,128]{3,2,1,0:T(8,128)(2,1)}, u32[]{:S(2)}) copy-start(bf16[1,64,64,128]{3,2,1,0:T(8,128)(2,1)} %param.5) | copy-start | bytes 3145732
  165.0 18.2 %collective-permute-start.13 = (bf16[1,1,64,128]{3,2,1,0:T(8,128)(2,1)S(1)}, bf16[1,1,64,128]{3,2,1,0:T(8,128)(2,1)S(1)}, u32[]{:S(2)}, u32[]{:S(2)}) collective-permute-start(bf16[1,1,64,128]{3,2,1,0:T(8,128)(2,1)S(1)} %slice.186), channel_id=1, source_target_pairs={{0,2},{2,4},{4,6},{1,3},{3,5},{5,7},{8,10},{10,12},{12,14},{9,11},... | collective-permute-start | bytes 49160 | tf_op jit(solution)/shard_map/ppermute | solution.py:37
  168.6 2.5 copy-start.4
  168.6 2.5 copy-start.10
  168.6 2.5 copy-start.15
  168.6 14.6 %collective-permute-start.14 = (bf16[1,1,64,128]{3,2,1,0:T(8,128)(2,1)S(1)}, bf16[1,1,64,128]{3,2,1,0:T(8,128)(2,1)S(1)}, u32[]{:S(2)}, u32[]{:S(2)}) collective-permute-start(bf16[1,1,64,128]{3,2,1,0:T(8,128)(2,1)S(1)} %slice.189), channel_id=1, source_target_pairs={{2,0},{4,2},{6,4},{3,1},{5,3},{7,5},{10,8},{12,10},{14,12},{11,9},... | collective-permute-start | bytes 49160 | tf_op jit(solution)/shard_map/ppermute | solution.py:39
  171.2 1.4 copy-start.17
  183.3 3.6 %collective-permute-start.15 = (bf16[1,66,1,128]{3,2,1,0:T(2,128)(2,1)S(1)}, bf16[1,66,1,128]{3,2,1,0:T(2,128)(2,1)S(1)}, u32[]{:S(2)}, u32[]{:S(2)}) collective-permute-start(bf16[1,66,1,128]{3,2,1,0:T(2,128)(2,1)S(1)} %get-tuple-element.11), channel_id=1, source_target_pairs={{0,1},{2,3},{4,5},{6,7},{8,9},{10,11},{12,13},{14,15},{16,17},{18,... | collective-permute-start | bytes 50696 | tf_op jit(solution)/shard_map/ppermute | solution.py:37
  184.6 3.1 collective-permute-start.16
  (6 other events, 6.1 us)
Sparse Core Ops, SparseCore 0:
  12.7 136.7 all-reduce.3
  192.8 131.7 all-reduce.5
